TPU v7x, 512 devices: a whole 4x4x16 slice. The times are simulated.
512 devices in a mesh: grp: 16 (over y, x), ch: 32 (over z, core).
Axes of the slice: x: 4, y: 4, z: 16, core: 2. Of those that a mesh axis runs over, the one named last changes fastest.
Arguments:
- x_in: bfloat16 [65536, 8192], P(('grp', 'ch')), may hold values from -6 to 6
- bc_in: bfloat16 [65536, 256], P(('grp', 'ch')), may hold values from -6 to 6
- dt_in: bfloat16 [65536, 128], P(('grp', 'ch')), may hold values from -2 to 14
- dt_bias: float32 [128], replicated, may hold values from -3 to -1
- a_log: float32 [128], P('ch'), may hold values from -7.5 to 0
- skip_d: float32 [128], P('ch'), may hold values from 0.5 to 1.5
- conv_x: float32 [4, 8192], P(None, 'ch'), may hold values from -3 to 3
- conv_x_bias: float32 [8192], P('ch'), may hold values from -3 to 3
- conv_bc: float32 [4, 256], replicated, may hold values from -3 to 3
- conv_bc_bias: float32 [256], replicated, may hold values from -3 to 3
- norm_gain: float32 [8192], replicated, may hold values from 0.5 to 1.5
- lengths: int32 [256], replicated, may hold values from 64 to 256, as said below
- dest_group: int32 [256], replicated, may hold values from -1 to 15, as said below
- dest_slot: int32 [256], replicated, may hold values from -1 to 15, as said below
Outputs:
- mixer_out: bfloat16 [65536, 8192], P(('grp', 'ch'))
Inputs may be any that keep to these rules, and one draw needn't show every extreme that they name: `dest_group`: -1 marks a dropped pair. From one group at most 2 surviving pairs go to any one group, and every group sends exactly 2 to some group; one group's pairs go to at most 8 groups. `dest_slot`: -1 exactly where dest_group is -1; no two surviving pairs share a destination group and slot. `lengths`: every group holds at least one pair of length 256.
All inputs are finite; a program needn't handle non-finite values.
Results may differ from a plain program's by a relative error of at most 0.0053.
Values may be sent and summed in bfloat16 or wider, within the bound.
No kernel may reach another device: no remote copies, remote signals or barrier semaphores. Data moves between devices by JAX's collectives and lax.ppermute only.
A program may use at most 64 MiB of HBM per device.

v0:
```python
import jax
import jax.numpy as jnp
from jax import lax
from jax.sharding import PartitionSpec as P

CAP = 2


def conv_silu(values, taps, bias):
    tap_count = taps.shape[0]
    length = values.shape[0]
    padded = jnp.concatenate(
        [jnp.zeros((tap_count - 1, values.shape[1]), jnp.float32), values], axis=0
    )
    total = jnp.zeros_like(values) + bias[None, :]
    for offset in range(tap_count):
        total = total + taps[offset][None, :] * padded[offset : offset + length]
    return jax.nn.silu(total)


def mix_pair(
    x_pair, bc_pair, step_pair, conv_x, conv_x_bias, conv_bc, conv_bc_bias, decay_rate, skip_gain
):
    length, chan_width = x_pair.shape
    head_count = decay_rate.shape[0]
    head_dim = chan_width // head_count
    state_dim = bc_pair.shape[1] // 2
    x_conv = conv_silu(x_pair.astype(jnp.float32), conv_x, conv_x_bias)
    bc_conv = conv_silu(bc_pair.astype(jnp.float32), conv_bc, conv_bc_bias)
    b_part = bc_conv[:, :state_dim]
    c_part = bc_conv[:, state_dim:]
    step_size = step_pair.astype(jnp.float32)
    log_decay = jnp.cumsum(-step_size * decay_rate[None, :], axis=0).T
    log_ratio = log_decay[:, :, None] - log_decay[:, None, :]
    later = jnp.arange(length, dtype=jnp.int32)[:, None]
    earlier = jnp.arange(length, dtype=jnp.int32)[None, :]
    causal = later >= earlier
    decay_mask = jnp.where(causal[None], jnp.exp(jnp.minimum(log_ratio, 0.0)), 0.0)
    scores = jnp.dot(
        c_part, b_part.T, precision=lax.Precision.HIGHEST, preferred_element_type=jnp.float32
    )
    weights = scores[None] * decay_mask * step_size.T[:, None, :]
    x_heads = x_conv.reshape(length, head_count, head_dim)
    mixed_out = jnp.einsum("hts,shp->thp", weights, x_heads, precision=lax.Precision.HIGHEST)
    mixed_out = mixed_out + skip_gain[None, :, None] * x_heads
    return mixed_out.reshape(length, chan_width).astype(jnp.bfloat16)


def route_plan(dest_group, dest_slot, my_group, n_grp, pair_count):
    by_group = dest_group.reshape(n_grp, pair_count)
    group_ids = jnp.arange(n_grp, dtype=jnp.int32)
    matches = (by_group[:, :, None] == group_ids[None, None, :]).astype(jnp.int32)
    earlier = jnp.cumsum(matches, axis=1) - matches
    ranking = jnp.sum(earlier * matches, axis=2)
    own_dest = by_group[my_group]
    own_rank = ranking[my_group]
    wanted = jnp.arange(n_grp * CAP, dtype=jnp.int32)
    wanted_group = wanted // CAP
    wanted_rank = wanted % CAP
    chosen = (own_dest[None, :] == wanted_group[:, None]) & (
        own_rank[None, :] == wanted_rank[:, None]
    )
    pair_ids = jnp.arange(pair_count, dtype=jnp.int32)
    send_index = jnp.where(
        jnp.any(chosen, axis=1),
        jnp.sum(chosen.astype(jnp.int32) * pair_ids[None, :], axis=1),
        pair_count,
    )
    arrivals = (dest_group[None, :] == my_group) & (dest_slot[None, :] == pair_ids[:, None])
    filled = jnp.any(arrivals, axis=1)
    all_ids = jnp.arange(n_grp * pair_count, dtype=jnp.int32)
    sources = jnp.sum(arrivals.astype(jnp.int32) * all_ids[None, :], axis=1)
    recv_index = sources // pair_count * CAP + ranking.reshape(-1)[sources]
    return (send_index, recv_index, filled)


def per_device(
    x_in,
    bc_in,
    dt_in,
    dt_bias,
    a_log,
    skip_d,
    conv_x,
    conv_x_bias,
    conv_bc,
    conv_bc_bias,
    norm_gain,
    lengths,
    dest_group,
    dest_slot,
):
    n_ch = lax.axis_size("ch")
    n_grp = lax.axis_size("grp")
    my_chan = lax.axis_index("ch")
    my_group = lax.axis_index("grp")
    tok_rows = x_in.shape[0]
    pair_len = 2 * tok_rows
    pair_count = n_ch * tok_rows // pair_len
    first_token = my_chan * tok_rows
    own_pair = my_group * pair_count + first_token // pair_len
    positions = first_token % pair_len + jnp.arange(tok_rows, dtype=jnp.int32)
    valid = positions < lengths[own_pair]
    x_masked = jnp.where(valid[:, None], x_in, jnp.zeros_like(x_in))
    bc_masked = jnp.where(valid[:, None], bc_in, jnp.zeros_like(bc_in))
    step_rows = (
        jax.nn.softplus(dt_in.astype(jnp.float32) + dt_bias[None, :])
        * valid[:, None].astype(jnp.float32)
    ).astype(jnp.bfloat16)
    x_chan, bc_cols, dt_chan = (
        lax.all_to_all(x_masked, "ch", split_axis=1, concat_axis=0, tiled=True),
        lax.all_to_all(bc_masked, "ch", split_axis=1, concat_axis=0, tiled=True),
        lax.all_to_all(step_rows, "ch", split_axis=1, concat_axis=0, tiled=True),
    )
    chan_width = x_chan.shape[1]
    head_local = dt_chan.shape[1]
    x_pairs = x_chan.reshape(pair_count, pair_len, chan_width)
    dt_pairs = dt_chan.reshape(pair_count, pair_len * head_local)
    decay_rate = jnp.exp(a_log)
    send_index, recv_index, filled = route_plan(dest_group, dest_slot, my_group, n_grp, pair_count)

    def outgoing(blocks):
        picked = jnp.take(blocks, send_index, axis=0, mode="fill", fill_value=0)
        return picked.reshape((n_grp, CAP) + blocks.shape[1:])

    def incoming(arrived):
        flat = arrived.reshape((n_grp * CAP,) + arrived.shape[2:])
        return jnp.take(flat, recv_index, axis=0)

    bc_col_pairs = bc_cols.reshape(pair_count, pair_len, bc_cols.shape[1])
    x_recv, bc_recv, dt_recv = (
        lax.all_to_all(outgoing(x_pairs), "grp", split_axis=0, concat_axis=0, tiled=True),
        lax.all_to_all(outgoing(bc_col_pairs), "grp", split_axis=0, concat_axis=0, tiled=True),
        lax.all_to_all(outgoing(dt_pairs), "grp", split_axis=0, concat_axis=0, tiled=True),
    )
    bc_whole = lax.all_gather(incoming(bc_recv), "ch", axis=2, tiled=True)

    def one_pair(pair_fragments):
        return mix_pair(
            pair_fragments[0],
            pair_fragments[1],
            pair_fragments[2].reshape(pair_len, head_local),
            conv_x,
            conv_x_bias,
            conv_bc,
            conv_bc_bias,
            decay_rate,
            skip_d,
        )

    mixed = lax.map(one_pair, (incoming(x_recv), bc_whole, incoming(dt_recv)))
    mixed = jnp.where(filled[:, None, None], mixed, jnp.zeros_like(mixed))
    returned = lax.all_to_all(
        mixed.reshape(pair_count * pair_len, chan_width),
        "ch",
        split_axis=0,
        concat_axis=1,
        tiled=True,
    )
    values = returned.astype(jnp.float32)
    scale = lax.rsqrt(jnp.mean(values * values, axis=1, keepdims=True) + 1e-05)
    return (values * scale * norm_gain[None, :]).astype(jnp.bfloat16)


def solution(mesh):
    placed = (
        P(("grp", "ch"), None),
        P(("grp", "ch"), None),
        P(("grp", "ch"), None),
        P(),
        P("ch"),
        P("ch"),
        P(None, "ch"),
        P("ch"),
        P(),
        P(),
        P(),
        P(),
        P(),
        P(),
    )
    return jax.shard_map(
        per_device, mesh=mesh, in_specs=placed, out_specs=P(("grp", "ch"), None), check_vma=False
    )
```

profile of v0, /device:TPU:1, one launch (start us, length us, event | category | flops | bytes accessed | tf_op | source)
XLA Modules:
  0.0 517.6 jit_solution(307897756995665700)
XLA Ops:
  6.5 0.9 copy.86
  7.5 1.3 dynamic_slice.22
  10.1 16.7 %all-to-all-start.2 = ((bf16[128,32,8]{0,2,1:T(8,128)(2,1)}), bf16[128,32,8]{0,2,1:T(8,128)(2,1)S(1)}, u32[]{:S(2)}, u32[]{:S(2)}) async-start(bf16[128,32,8]{0,2,1:T(8,128)(2,1)} %select_bitcast_fusion), calls=%async_computation.2 | async-start | bytes 131072 | tf_op jit(solution)/shard_map/all_to_all | solution.py:112
  28.7 3.2 copy.84
  32.8 7.1 %all-to-all-done.2 = bf16[128,32,8]{0,2,1:T(8,128)(2,1)S(1)} async-done(((bf16[128,32,8]{0,2,1:T(8,128)(2,1)}), bf16[128,32,8]{0,2,1:T(8,128)(2,1)S(1)}, u32[]{:S(2)}, u32[]{:S(2)}) %all-to-all-start.2) | async-done | bytes 65568 | tf_op jit(solution)/shard_map/all_to_all | solution.py:112
  39.8 5.1 all-to-all-start.4
  46.3 10.8 %all-to-all-done.4 = bf16[128,32,4]{0,2,1:T(4,128)(2,1)S(1)} async-done(((bf16[128,32,4]{0,2,1:T(4,128)(2,1)}), bf16[128,32,4]{0,2,1:T(4,128)(2,1)S(1)}, u32[]{:S(2)}, u32[]{:S(2)}) %all-to-all-start.4) | async-done | bytes 32800 | tf_op jit(solution)/shard_map/all_to_all | solution.py:113
  57.1 6.8 %all-to-all-start.3 = ((bf16[16,2,256,8]{2,3,1,0:T(8,128)(2,1)}), bf16[16,2,256,8]{2,3,1,0:T(8,128)(2,1)S(1)}, u32[]{:S(2)}, u32[]{:S(2)}) async-start(bf16[16,2,256,8]{2,3,1,0:T(8,128)(2,1)} %broadcast_select_fusion.5), calls=%async_computation.3 | async-start | bytes 262144 | tf_op jit(solution)/shard_map/all_to_all | solution.py:133
  63.8 1.5 broadcast_select_fusion.3
  65.3 5.5 %all-to-all-done.3 = bf16[16,2,256,8]{2,3,1,0:T(8,128)(2,1)S(1)} async-done(((bf16[16,2,256,8]{2,3,1,0:T(8,128)(2,1)}), bf16[16,2,256,8]{2,3,1,0:T(8,128)(2,1)S(1)}, u32[]{:S(2)}, u32[]{:S(2)}) %all-to-all-start.3) | async-done | bytes 131104 | tf_op jit(solution)/shard_map/all_to_all | solution.py:133
  70.8 6.3 %all-to-all-start = ((bf16[128,32,256]{0,2,1:T(8,128)(2,1)}), bf16[128,32,256]{0,2,1:T(8,128)(2,1)S(1)}, u32[]{:S(2)}, u32[]{:S(2)}) async-start(bf16[128,32,256]{0,2,1:T(8,128)(2,1)} %bitcast.147), calls=%async_computation | async-start | bytes 4194304 | tf_op jit(solution)/shard_map/all_to_all | solution.py:111
  78.6 2.0 reshape.292
  82.6 93.4 %all-to-all-done = bf16[128,32,256]{0,2,1:T(8,128)(2,1)S(1)} async-done(((bf16[128,32,256]{0,2,1:T(8,128)(2,1)}), bf16[128,32,256]{0,2,1:T(8,128)(2,1)S(1)}, u32[]{:S(2)}, u32[]{:S(2)}) %all-to-all-start) | async-done | bytes 2097184 | tf_op jit(solution)/shard_map/all_to_all | solution.py:111
  176.0 3.5 all-to-all-start.5
  179.5 3.3 copy.85
  182.7 2.8 gather_fusion.1
  185.5 4.5 broadcast_select_fusion
  190.0 6.8 %all-to-all-start.1 = ((bf16[16,2,256,256]{3,2,1,0:T(8,128)(2,1)}), bf16[16,2,256,256]{3,2,1,0:T(8,128)(2,1)}, u32[]{:S(2)}, u32[]{:S(2)}) async-start(bf16[16,2,256,256]{3,2,1,0:T(8,128)(2,1)} %broadcast_select_fusion), calls=%async_computation.1 | async-start | bytes 8388608 | tf_op jit(solution)/shard_map/all_to_all | solution.py:132
  198.4 53.1 %all-to-all-done.1 = bf16[16,2,256,256]{3,2,1,0:T(8,128)(2,1)} async-done(((bf16[16,2,256,256]{3,2,1,0:T(8,128)(2,1)}), bf16[16,2,256,256]{3,2,1,0:T(8,128)(2,1)}, u32[]{:S(2)}, u32[]{:S(2)}) %all-to-all-start.1) | async-done | bytes 4194336 | tf_op jit(solution)/shard_map/all_to_all | solution.py:132
  251.6 2.9 gather_fusion.2
  254.5 1.6 broadcast_select_fusion.1
  256.1 11.1 %all-gather.2.cloned.1.call-done = bf16[16,256,256]{1,2,0:T(8,128)(2,1)} async-done(((bf16[16,256,8]{1,2,0:T(8,128)(2,1)}), bf16[16,256,256]{1,2,0:T(8,128)(2,1)}) %all-gather.2.cloned.1.call-update) | async-done | bytes 2097168 | tf_op jit(solution)/shard_map/all_gather | solution.py:136
  267.2 119.3 %while.11 = (s32[]{:T(128)}, bf16[16,256,256]{2,1,0:T(8,128)(2,1)}, f32[256]{0:T(256)S(1)}, f32[4,256]{1,0:T(4,128)S(1)}, bf16[16,256,256]{2,1,0:T(8,128)(2,1)},...) while((s32[]{:T(128)}, bf16[16,256,256]{2,1,0:T(8,128)(2,1)}, ...), condition=%wide.region_9.10_spmd.clone, body=%wide.region_6.9_spmd.sunk.clone | while | flops 305400832 | bytes 4293649 | solution.py:151
  270.8 1.2 reduce-window.14
  272.5 1.4 fusion.74
  275.7 0.9 bitcast_convert_fusion.6
  278.2 1.2 reduce-window.14
  280.0 1.4 fusion.74
  283.2 0.9 bitcast_convert_fusion.6
  285.7 1.2 reduce-window.14
  287.4 1.4 fusion.74
  290.6 0.9 bitcast_convert_fusion.6
  293.1 1.2 reduce-window.14
  294.9 1.4 fusion.74
  300.6 1.2 reduce-window.14
  302.3 1.4 fusion.74
  308.0 1.2 reduce-window.14
  309.8 1.4 fusion.74
  315.5 1.2 reduce-window.14
  317.2 1.4 fusion.74
  322.9 1.2 reduce-window.14
  324.7 1.4 fusion.74
  330.4 1.2 reduce-window.14
  332.1 1.4 fusion.74
  337.9 1.2 reduce-window.14
  339.6 1.4 fusion.74
  345.3 1.2 reduce-window.14
  347.0 1.4 fusion.74
  352.8 1.2 reduce-window.14
  354.5 1.4 fusion.74
  360.2 1.2 reduce-window.14
  361.9 1.4 fusion.74
  367.7 1.2 reduce-window.14
  369.4 1.4 fusion.74
  375.1 1.2 reduce-window.14
  376.9 1.4 fusion.74
  382.6 1.2 reduce-window.14
  384.3 1.4 fusion.74
  386.5 1.8 broadcast_select_fusion.2
  388.3 107.9 %all_to_all.76 = bf16[32,128,256]{2,1,0:T(8,128)(2,1)S(1)} all-to-all(bf16[32,128,256]{2,1,0:T(8,128)(2,1)S(1)} %bitcast.148), channel_id=1, replica_groups=mesh['grp'=16,'ch'=32] {'ch'}, dimensions={0} | all-to-all | bytes 4194304 | tf_op jit(solution)/shard_map/all_to_all | solution.py:153
  496.2 2.4 convert_bitcast_fusion
  498.7 5.6 %copy.92 = f32[128,32,256]{0,2,1:T(8,128)} copy(f32[128,32,256]{2,0,1:T(8,128)} %convert_bitcast_fusion) | data formatting | bytes 8388608 | tf_op jit(solution)/shard_map/convert_element_type | solution.py:160
  505.0 2.8 fusion.34
  507.8 2.9 copy.93
  (434 shorter events, 84.4 us)
Async XLA Ops:
  10.1 29.8 %all-to-all-start.2 = ((bf16[128,32,8]{0,2,1:T(8,128)(2,1)}), bf16[128,32,8]{0,2,1:T(8,128)(2,1)S(1)}, u32[]{:S(2)}, u32[]{:S(2)}) async-start(bf16[128,32,8]{0,2,1:T(8,128)(2,1)} %select_bitcast_fusion), calls=%async_computation.2 | async-start | bytes 131072 | tf_op jit(solution)/shard_map/all_to_all | solution.py:112
  28.6 3.3 copy-start.4
  28.6 3.4 copy-start.9
  39.8 17.3 %all-to-all-start.4 = ((bf16[128,32,4]{0,2,1:T(4,128)(2,1)}), bf16[128,32,4]{0,2,1:T(4,128)(2,1)S(1)}, u32[]{:S(2)}, u32[]{:S(2)}) async-start(bf16[128,32,4]{0,2,1:T(4,128)(2,1)} %bitcast.37), calls=%async_computation.4 | async-start | bytes 65536 | tf_op jit(solution)/shard_map/all_to_all | solution.py:113
  57.1 13.7 %all-to-all-start.3 = ((bf16[16,2,256,8]{2,3,1,0:T(8,128)(2,1)}), bf16[16,2,256,8]{2,3,1,0:T(8,128)(2,1)S(1)}, u32[]{:S(2)}, u32[]{:S(2)}) async-start(bf16[16,2,256,8]{2,3,1,0:T(8,128)(2,1)} %broadcast_select_fusion.5), calls=%async_computation.3 | async-start | bytes 262144 | tf_op jit(solution)/shard_map/all_to_all | solution.py:133
  70.8 6.4 %copy-start.7 = (s32[256]{0:T(256)S(1)}, s32[256]{0:T(256)}, u32[]{:S(2)}) copy-start(s32[256]{0:T(256)} %param.28) | copy-start | bytes 3076
  70.8 6.4 %copy-start.8 = (s32[256]{0:T(256)S(1)}, s32[256]{0:T(256)}, u32[]{:S(2)}) copy-start(s32[256]{0:T(256)} %param.29) | copy-start | bytes 3076
  70.8 105.2 %all-to-all-start = ((bf16[128,32,256]{0,2,1:T(8,128)(2,1)}), bf16[128,32,256]{0,2,1:T(8,128)(2,1)S(1)}, u32[]{:S(2)}, u32[]{:S(2)}) async-start(bf16[128,32,256]{0,2,1:T(8,128)(2,1)} %bitcast.147), calls=%async_computation | async-start | bytes 4194304 | tf_op jit(solution)/shard_map/all_to_all | solution.py:111
  176.0 3.5 copy-start
  176.0 14.0 %all-to-all-start.5 = ((bf16[16,2,1024]{2,1,0:T(2,128)(2,1)}), bf16[16,2,1024]{2,1,0:T(2,128)(2,1)S(1)}, u32[]{:S(2)}, u32[]{:S(2)}) async-start(bf16[16,2,1024]{2,1,0:T(2,128)(2,1)} %broadcast_select_fusion.4), calls=%async_computation.5 | async-start | bytes 131072 | tf_op jit(solution)/shard_map/all_to_all | solution.py:134
  190.0 7.6 %copy-start.10 = (f32[4]{0:T(128)S(1)}, f32[4]{0:T(128)}, u32[]{:S(2)}) copy-start(f32[4]{0:T(128)} %param.20) | copy-start | bytes 52
  190.0 61.6 %all-to-all-start.1 = ((bf16[16,2,256,256]{3,2,1,0:T(8,128)(2,1)}), bf16[16,2,256,256]{3,2,1,0:T(8,128)(2,1)}, u32[]{:S(2)}, u32[]{:S(2)}) async-start(bf16[16,2,256,256]{3,2,1,0:T(8,128)(2,1)} %broadcast_select_fusion), calls=%async_computation.1 | async-start | bytes 8388608 | tf_op jit(solution)/shard_map/all_to_all | solution.py:132
  196.8 70.4 %all-gather.2.cloned.1.call-start = ((), (), s32[]{:S(2)}) async-start(), calls=%async_computation.7 | async-start | bytes 2162688 | tf_op jit(solution)/shard_map/all_gather | solution.py:136
  254.5 12.7 %copy-start.1 = (f32[4,256]{1,0:T(4,128)S(1)}, f32[4,256]{1,0:T(4,128)}, u32[]{:S(2)}) copy-start(f32[4,256]{1,0:T(4,128)} %param.22) | copy-start | bytes 12292
  254.5 12.7 %copy-start.2 = (f32[4,256]{1,0:T(4,128)S(1)}, f32[4,256]{1,0:T(4,128)}, u32[]{:S(2)}) copy-start(f32[4,256]{1,0:T(4,128)} %param.24) | copy-start | bytes 12292
  254.5 12.7 %copy-start.5 = (f32[256]{0:T(256)S(1)}, f32[256]{0:T(256)}, u32[]{:S(2)}) copy-start(f32[256]{0:T(256)} %param.23) | copy-start | bytes 3076
  254.5 12.7 %copy-start.6 = (f32[256]{0:T(256)S(1)}, f32[256]{0:T(256)}, u32[]{:S(2)}) copy-start(f32[256]{0:T(256)} %param.25) | copy-start | bytes 3076
  254.5 12.7 %copy-start.11 = (f32[4]{0:T(128)S(1)}, f32[4]{0:T(128)}, u32[]{:S(2)}) copy-start(f32[4]{0:T(128)} %param.21) | copy-start | bytes 52
  504.2 0.8 copy-start.3
Sparse Core Ops, SparseCore 0:
  199.6 67.5 all-gather.1
where the time goes:
time: 519 us; the launch traced here: 518 us
  waiting for transfers between devices  181 us (35%)
  blocking collectives  108 us (21%)
  other arithmetic  71.4 us (14%)
  local copies, waits for them, and re-layouts  68 us (13%)
  starting transfers between devices  45.2 us (9%)
  matrix products  28.8 us (6%)
  between operations  13.7 us (3%)
    all_to_all x1, blocking collectives, per_device(): lax.all_to_all(mixed.reshape(pair_count * pair_len, chan_width), 'ch', sp...  108 us
    all_to_all x1, waiting for transfers between devices, per_device(): lax.all_to_all(x_masked, 'ch', split_axis=1, concat_axis=0, tiled=True)  93.4 us
    all_to_all x1, waiting for transfers between devices, per_device(): lax.all_to_all(outgoing(x_pairs), 'grp', split_axis=0, concat_axis=0, til...  53.1 us
    dot_general x16, matrix products, mix_pair(): jnp.einsum('hts,shp->thp', weights, x_heads, precision=lax.Precision.HIGH...  22.2 us
    another operation x33, other arithmetic  20 us
    all_to_all x1, starting transfers between devices, per_device(): lax.all_to_all(bc_masked, 'ch', split_axis=1, concat_axis=0, tiled=True)  16.7 us
    dynamic_slice x32, local copies, waits for them, and re-layouts, per_device(): mixed = lax.map(one_pair, (incoming(x_recv), bc_whole, incoming(dt_recv)))  16.2 us
    convert_element_type x16, other arithmetic, mix_pair(): bc_conv = conv_silu(bc_pair.astype(jnp.float32), conv_bc, conv_bc_bias)  14.9 us
  transfers between devices with their start and end apart: 7, of which 6 were waited for; matrix products, arithmetic and copies ran while one was open for 6% of the time, Pallas kernels for 0%

commit v1 on v0

--- a/solution.py
+++ b/solution.py
@@ -4,6 +4,13 @@
 from jax.sharding import PartitionSpec as P
 
 CAP = 2
+
+
+def gather_over(x, mesh_axis, d):
+    size = lax.axis_size(mesh_axis)
+    pieces = jnp.stack([x for _ in range(size)])
+    pieces = lax.all_to_all(pieces, mesh_axis, split_axis=0, concat_axis=0)
+    return jnp.concatenate(pieces, axis=d)
 
 
 def conv_silu(values, taps, bias):
@@ -133,7 +140,7 @@
         lax.all_to_all(outgoing(bc_col_pairs), "grp", split_axis=0, concat_axis=0, tiled=True),
         lax.all_to_all(outgoing(dt_pairs), "grp", split_axis=0, concat_axis=0, tiled=True),
     )
-    bc_whole = lax.all_gather(incoming(bc_recv), "ch", axis=2, tiled=True)
+    bc_whole = gather_over(incoming(bc_recv), "ch", 2)
 
     def one_pair(pair_fragments):
         return mix_pair(

time: 519 us -> 603 us (1.16)
  waiting for transfers between devices: 181 us -> 268 us
  between operations: 13.7 us -> 0.31 us
    all_to_all x0 -> x1, waiting for transfers between devices: none -> 87.9 us  [gather_over(): pieces = lax.all_to_all(pieces, mesh_axis, split_axis=0, concat_axis=0)]
    all_to_all x1, starting transfers between devices: 16.7 us -> 4.66 us  [per_device(): lax.all_to_all(bc_masked, 'ch', split_axis=1, concat_axis=0, tiled=True)]
    all_to_all x1, starting transfers between devices: 5.12 us -> 16.7 us  [per_device(): lax.all_to_all(step_rows, 'ch', split_axis=1, concat_axis=0, tiled=True)]
    all_gather x1 -> x0, waiting for transfers between devices: 11.1 us -> none  [per_device(): bc_whole = lax.all_gather(incoming(bc_recv), 'ch', axis=2, tiled=True)]
  transfers between devices with their start and end apart: 7 -> 7, of which waited for: 6 -> 7; matrix products, arithmetic and copies ran while one was open for 6% -> 5% of each run, Pallas kernels for 0% -> 0%
where the time goes in v1:
time: 603 us; the launch traced here: 602 us
  waiting for transfers between devices  268 us (44%)
  blocking collectives  107 us (18%)
  local copies, waits for them, and re-layouts  74 us (12%)
  other arithmetic  71.4 us (12%)
  starting transfers between devices  50.8 us (8%)
  matrix products  28.8 us (5%)
    all_to_all x1, blocking collectives, per_device(): lax.all_to_all(mixed.reshape(pair_count * pair_len, chan_width), 'ch', sp...  107 us
    all_to_all x1, waiting for transfers between devices, per_device(): lax.all_to_all(x_masked, 'ch', split_axis=1, concat_axis=0, tiled=True)  96.6 us
    all_to_all x1, waiting for transfers between devices, gather_over(): pieces = lax.all_to_all(pieces, mesh_axis, split_axis=0, concat_axis=0)  87.9 us
    all_to_all x1, waiting for transfers between devices, per_device(): lax.all_to_all(outgoing(x_pairs), 'grp', split_axis=0, concat_axis=0, til...  58.4 us
    dot_general x16, matrix products, mix_pair(): jnp.einsum('hts,shp->thp', weights, x_heads, precision=lax.Precision.HIGH...  22.2 us
    another operation x33, other arithmetic  20 us
    all_to_all x1, starting transfers between devices, per_device(): lax.all_to_all(step_rows, 'ch', split_axis=1, concat_axis=0, tiled=True)  16.7 us
    dynamic_slice x32, local copies, waits for them, and re-layouts, per_device(): mixed = lax.map(one_pair, (incoming(x_recv), bc_whole, incoming(dt_recv)))  16.2 us
  transfers between devices with their start and end apart: 7, of which 7 were waited for; matrix products, arithmetic and copies ran while one was open for 5% of the time, Pallas kernels for 0%

profile of v1, /device:TPU:1, one launch (start us, length us, event | category | flops | bytes accessed | tf_op | source)
XLA Modules:
  0.0 601.6 jit_solution(13695391256754699704)
XLA Ops:
  0.9 1.3 dynamic_slice.22
  2.8 1.4 fusion.38
  4.2 16.7 %all-to-all-start.5 = ((bf16[128,32,4]{0,2,1:T(4,128)(2,1)}), bf16[128,32,4]{0,2,1:T(4,128)(2,1)S(1)}, u32[]{:S(2)}, u32[]{:S(2)}) async-start(bf16[128,32,4]{0,2,1:T(4,128)(2,1)} %bitcast.39), calls=%async_computation.5 | async-start | bytes 65536 | tf_op jit(solution)/shard_map/all_to_all | solution.py:120
  24.3 8.6 %all-to-all-done.5 = bf16[128,32,4]{0,2,1:T(4,128)(2,1)S(1)} async-done(((bf16[128,32,4]{0,2,1:T(4,128)(2,1)}), bf16[128,32,4]{0,2,1:T(4,128)(2,1)S(1)}, u32[]{:S(2)}, u32[]{:S(2)}) %all-to-all-start.5) | async-done | bytes 32800 | tf_op jit(solution)/shard_map/all_to_all | solution.py:120
  33.0 4.7 all-to-all-start.2
  37.7 3.2 copy.85
  41.4 2.0 reshape.302
  44.8 5.8 all-to-all-done.2
  50.7 6.8 %all-to-all-start.6 = ((bf16[16,2,1024]{2,1,0:T(2,128)(2,1)}), bf16[16,2,1024]{2,1,0:T(2,128)(2,1)S(1)}, u32[]{:S(2)}, u32[]{:S(2)}) async-start(bf16[16,2,1024]{2,1,0:T(2,128)(2,1)} %broadcast_select_fusion.4), calls=%async_computation.6 | async-start | bytes 131072 | tf_op jit(solution)/shard_map/all_to_all | solution.py:141
  58.8 5.2 all-to-all-done.6
  64.0 3.5 all-to-all-start.3
  67.5 1.5 broadcast_select_fusion.3
  69.0 5.3 all-to-all-done.3
  74.3 9.1 %all-to-all-start = ((bf16[128,32,256]{0,2,1:T(8,128)(2,1)}), bf16[128,32,256]{0,2,1:T(8,128)(2,1)S(1)}, u32[]{:S(2)}, u32[]{:S(2)}) async-start(bf16[128,32,256]{0,2,1:T(8,128)(2,1)} %bitcast.152), calls=%async_computation | async-start | bytes 4194304 | tf_op jit(solution)/shard_map/all_to_all | solution.py:118
  85.1 96.6 %all-to-all-done = bf16[128,32,256]{0,2,1:T(8,128)(2,1)S(1)} async-done(((bf16[128,32,256]{0,2,1:T(8,128)(2,1)}), bf16[128,32,256]{0,2,1:T(8,128)(2,1)S(1)}, u32[]{:S(2)}, u32[]{:S(2)}) %all-to-all-start) | async-done | bytes 2097184 | tf_op jit(solution)/shard_map/all_to_all | solution.py:118
  181.7 1.8 stack.2
  183.7 5.5 all-to-all-start.4
  189.2 3.3 copy.86
  192.5 2.8 gather_fusion.1
  195.3 4.5 broadcast_select_fusion
  199.8 87.9 %all-to-all-done.4 = bf16[32,16,256,8]{2,3,1,0:T(8,128)(2,1)} async-done(((bf16[32,16,256,8]{2,3,1,0:T(8,128)(2,1)}), bf16[32,16,256,8]{2,3,1,0:T(8,128)(2,1)}, u32[]{:S(2)}, u32[]{:S(2)}) %all-to-all-start.4) | async-done | bytes 2097184 | tf_op jit(solution)/shard_map/all_to_all | solution.py:12
  287.6 4.5 all-to-all-start.1
  293.0 3.2 copy.103
  296.2 58.4 %all-to-all-done.1 = bf16[16,2,256,256]{3,2,1,0:T(8,128)(2,1)} async-done(((bf16[16,2,256,256]{3,2,1,0:T(8,128)(2,1)}), bf16[16,2,256,256]{3,2,1,0:T(8,128)(2,1)}, u32[]{:S(2)}, u32[]{:S(2)}) %all-to-all-start.1) | async-done | bytes 4194336 | tf_op jit(solution)/shard_map/all_to_all | solution.py:139
  354.6 2.9 gather_fusion.2
  357.6 1.6 broadcast_select_fusion.1
  359.2 119.3 %while.11 = (s32[]{:T(128)}, bf16[16,256,256]{2,1,0:T(8,128)(2,1)}, f32[256]{0:T(256)S(1)}, f32[4,256]{1,0:T(4,128)S(1)}, bf16[16,256,256]{2,1,0:T(8,128)(2,1)},...) while((s32[]{:T(128)}, bf16[16,256,256]{2,1,0:T(8,128)(2,1)}, ...), condition=%wide.region_9.10_spmd.clone, body=%wide.region_6.9_spmd.sunk.clone | while | flops 305400832 | bytes 4293649 | solution.py:158
  362.8 1.2 reduce-window.14
  364.5 1.4 fusion.74
  370.2 1.2 reduce-window.14
  372.0 1.4 fusion.74
  377.7 1.2 reduce-window.14
  379.4 1.4 fusion.74
  385.1 1.2 reduce-window.14
  386.9 1.4 fusion.74
  392.6 1.2 reduce-window.14
  394.3 1.4 fusion.74
  400.0 1.2 reduce-window.14
  401.8 1.4 fusion.74
  407.5 1.2 reduce-window.14
  409.2 1.4 fusion.74
  414.9 1.2 reduce-window.14
  416.7 1.4 fusion.74
  422.4 1.2 reduce-window.14
  424.1 1.4 fusion.74
  429.9 1.2 reduce-window.14
  431.6 1.4 fusion.74
  437.3 1.2 reduce-window.14
  439.0 1.4 fusion.74
  444.8 1.2 reduce-window.14
  446.5 1.4 fusion.74
  452.2 1.2 reduce-window.14
  453.9 1.4 fusion.74
  459.7 1.2 reduce-window.14
  461.4 1.4 fusion.74
  467.1 1.2 reduce-window.14
  468.9 1.4 fusion.74
  476.3 1.4 fusion.74
  478.5 1.8 broadcast_select_fusion.2
  480.3 106.8 %all_to_all.81 = bf16[32,128,256]{2,1,0:T(8,128)(2,1)S(1)} all-to-all(bf16[32,128,256]{2,1,0:T(8,128)(2,1)S(1)} %bitcast.153), channel_id=1, replica_groups=mesh['grp'=16,'ch'=32] {'ch'}, dimensions={0} | all-to-all | bytes 4194304 | tf_op jit(solution)/shard_map/all_to_all | solution.py:160
  587.1 2.4 convert_bitcast_fusion
  589.5 5.6 copy.94
  595.9 2.8 fusion.34
  598.7 2.9 copy.95
  (431 shorter events, 88.9 us)
Async XLA Ops:
  4.2 28.8 %all-to-all-start.5 = ((bf16[128,32,4]{0,2,1:T(4,128)(2,1)}), bf16[128,32,4]{0,2,1:T(4,128)(2,1)S(1)}, u32[]{:S(2)}, u32[]{:S(2)}) async-start(bf16[128,32,4]{0,2,1:T(4,128)(2,1)} %bitcast.39), calls=%async_computation.5 | async-start | bytes 65536 | tf_op jit(solution)/shard_map/all_to_all | solution.py:120
  33.0 17.7 %all-to-all-start.2 = ((bf16[128,32,8]{0,2,1:T(8,128)(2,1)}), bf16[128,32,8]{0,2,1:T(8,128)(2,1)S(1)}, u32[]{:S(2)}, u32[]{:S(2)}) async-start(bf16[128,32,8]{0,2,1:T(8,128)(2,1)} %select_bitcast_fusion), calls=%async_computation.2 | async-start | bytes 131072 | tf_op jit(solution)/shard_map/all_to_all | solution.py:119
  50.7 13.3 %all-to-all-start.6 = ((bf16[16,2,1024]{2,1,0:T(2,128)(2,1)}), bf16[16,2,1024]{2,1,0:T(2,128)(2,1)S(1)}, u32[]{:S(2)}, u32[]{:S(2)}) async-start(bf16[16,2,1024]{2,1,0:T(2,128)(2,1)} %broadcast_select_fusion.4), calls=%async_computation.6 | async-start | bytes 131072 | tf_op jit(solution)/shard_map/all_to_all | solution.py:141
  64.0 10.3 %all-to-all-start.3 = ((bf16[16,2,256,8]{2,3,1,0:T(8,128)(2,1)}), bf16[16,2,256,8]{2,3,1,0:T(8,128)(2,1)S(1)}, u32[]{:S(2)}, u32[]{:S(2)}) async-start(bf16[16,2,256,8]{2,3,1,0:T(8,128)(2,1)} %broadcast_select_fusion.5), calls=%async_computation.3 | async-start | bytes 262144 | tf_op jit(solution)/shard_map/all_to_all | solution.py:140
  74.3 9.3 %copy-start.6 = (s32[256]{0:T(256)S(1)}, s32[256]{0:T(256)}, u32[]{:S(2)}) copy-start(s32[256]{0:T(256)} %param.28) | copy-start | bytes 3076
  74.3 9.3 %copy-start.7 = (s32[256]{0:T(256)S(1)}, s32[256]{0:T(256)}, u32[]{:S(2)}) copy-start(s32[256]{0:T(256)} %param.29) | copy-start | bytes 3076
  74.3 107.4 %all-to-all-start = ((bf16[128,32,256]{0,2,1:T(8,128)(2,1)}), bf16[128,32,256]{0,2,1:T(8,128)(2,1)S(1)}, u32[]{:S(2)}, u32[]{:S(2)}) async-start(bf16[128,32,256]{0,2,1:T(8,128)(2,1)} %bitcast.152), calls=%async_computation | async-start | bytes 4194304 | tf_op jit(solution)/shard_map/all_to_all | solution.py:118
  181.7 2.0 copy-start
  183.7 103.9 %all-to-all-start.4 = ((bf16[32,16,256,8]{2,3,1,0:T(8,128)(2,1)}), bf16[32,16,256,8]{2,3,1,0:T(8,128)(2,1)}, u32[]{:S(2)}, u32[]{:S(2)}) async-start(bf16[32,16,256,8]{2,3,1,0:T(8,128)(2,1)} %stack.2), calls=%async_computation.4 | async-start | bytes 4194304 | tf_op jit(solution)/shard_map/all_to_all | solution.py:12
  199.8 92.4 %copy-start.8 = (f32[4]{0:T(128)S(1)}, f32[4]{0:T(128)}, u32[]{:S(2)}) copy-start(f32[4]{0:T(128)} %param.20) | copy-start | bytes 52
  287.6 67.0 %all-to-all-start.1 = ((bf16[16,2,256,256]{3,2,1,0:T(8,128)(2,1)}), bf16[16,2,256,256]{3,2,1,0:T(8,128)(2,1)}, u32[]{:S(2)}, u32[]{:S(2)}) async-start(bf16[16,2,256,256]{3,2,1,0:T(8,128)(2,1)} %broadcast_select_fusion), calls=%async_computation.1 | async-start | bytes 8388608 | tf_op jit(solution)/shard_map/all_to_all | solution.py:139
  357.5 1.7 copy-start.1
  357.5 1.7 copy-start.2
  357.5 1.7 copy-start.4
  357.6 1.7 copy-start.5
  357.6 1.6 copy-start.9
  595.1 0.8 copy-start.3
